TPU v7x, 32 devices: a whole 2x2x4 slice. The times are simulated.
32 devices in a mesh: row: 4 (over x, core), col: 8 (over z, y).
Axes of the slice: x: 2, y: 2, z: 4, core: 2. Of those that a mesh axis runs over, the one named last changes fastest.
Arguments:
- embeddings: bfloat16 [4096, 512], P(('row', 'col')), may hold values from -6 to 6
- sketch: bfloat16 [4096, 64], P(('row', 'col')), may hold values from -240 to 240
Outputs:
- basis: float32 [4096, 64], P(('row', 'col'))
- first_pass: float32 [4096, 64], P(('row', 'col'))
All inputs are finite; a program needn't handle non-finite values.
Results may differ from a plain program's by a relative error of at most 0.00205.
Values may be sent and summed in bfloat16 or wider, within the bound.
No kernel may reach another device: no remote copies, remote signals or barrier semaphores. Data moves between devices by JAX's collectives and lax.ppermute only.
A program may use at most 64 MiB of HBM per device.

v0:
```python
import jax
import jax.numpy as jnp
from jax import lax
from jax.sharding import PartitionSpec as P


def squares_of(points):
    return jnp.sum(jnp.square(points.astype(jnp.float32)), axis=1)


def kernel_tile(left, right, left_sq, right_sq, gamma):
    cross = lax.dot_general(
        left, right, (((1,), (1,)), ((), ())), preferred_element_type=jnp.float32
    )
    dist = left_sq[:, None] + right_sq[None, :] - 2.0 * cross
    return jnp.exp(-gamma * dist).astype(jnp.bfloat16)


def product_of(left, right):
    return lax.dot_general(
        left,
        right,
        (((0,), (0,)), ((), ())),
        precision=lax.Precision.HIGHEST,
        preferred_element_type=jnp.float32,
    )


def per_device(embeddings, sketch):
    width = embeddings.shape[1]
    gamma = 3.0 / width
    own_points = lax.all_gather(embeddings, "row", axis=0, tiled=True)
    own_sq = squares_of(own_points)
    empty = jnp.zeros((own_points.shape[0], sketch.shape[1]), jnp.float32)
    total = empty
    points = lax.all_gather(embeddings, "col", axis=0, tiled=True)
    tests = lax.all_gather(sketch, "col", axis=0, tiled=True)
    count = points.shape[0]
    size = 512

    def step(carry, block):
        block_points, block_tests = block
        tile = kernel_tile(own_points, block_points, own_sq, squares_of(block_points), gamma)
        return (carry + jnp.dot(tile, block_tests, preferred_element_type=jnp.float32), None)

    stacked = (
        points.reshape(count // size, size, width),
        tests.reshape(count // size, size, tests.shape[1]),
    )
    total, unused = lax.scan(step, total, stacked)
    sketched = lax.psum_scatter(total, "row", scatter_dimension=0, tiled=True)
    core = lax.psum(product_of(sketch.astype(jnp.float32), sketched), ("row", "col"))
    lower = jnp.linalg.cholesky(core)
    first = jax.scipy.linalg.solve_triangular(lower, sketched.T, lower=True).T
    gram_two = lax.psum(product_of(first, first), ("row", "col"))
    lower_two = jnp.linalg.cholesky(gram_two)
    second = jax.scipy.linalg.solve_triangular(lower_two, first.T, lower=True).T
    total_points = sketched.shape[0] * lax.axis_size("row") * lax.axis_size("col")
    scale = jnp.sqrt(jnp.float32(total_points))
    return (second * scale, first * scale)


def solution(mesh):
    placed = (P(("row", "col"), None), P(("row", "col"), None))
    return jax.shard_map(
        per_device,
        mesh=mesh,
        in_specs=placed,
        out_specs=(P(("row", "col"), None), P(("row", "col"), None)),
        check_vma=False,
    )
```

profile of v0, /device:TPU:0, one launch (start us, length us, event | category | flops | bytes accessed | tf_op | source)
XLA Modules:
  0.0 193.4 jit_solution(8559707278417701284)
XLA Ops:
  7.2 0.7 all-gather.2.cloned.1.call-update
  7.9 0.0 reduce-scatter.2.cloned.1.call-start
  8.0 28.2 %all_gather.11 = bf16[1024,64]{0,1:T(8,128)(2,1)S(1)} all-gather(bf16[128,64]{0,1:T(8,128)(2,1)S(1)} %copy-done.3), channel_id=1, replica_groups=mesh['row'=4,'col'=8] {'col'}, dimensions={0}, use_global_device_ids=true | all-gather | bytes 147456 | tf_op jit(solution)/shard_map/all_gather | solution.py:37
  36.2 0.2 copy.4
  36.4 0.7 copy-done
  37.1 7.2 %all_gather.9 = bf16[512,512]{1,0:T(8,128)(2,1)S(1)} all-gather(bf16[128,512]{1,0:T(8,128)(2,1)S(1)} %copy-done), channel_id=1, replica_groups=mesh['row'=4,'col'=8] {'row'}, dimensions={0}, use_global_device_ids=true | all-gather | bytes 655360 | tf_op jit(solution)/shard_map/all_gather | solution.py:32
  44.3 0.2 multiply_reduce_fusion.1
  44.5 9.1 %all-gather.2.cloned.1.call-done = bf16[1024,512]{1,0:T(8,128)(2,1)} async-done(((bf16[128,512]{1,0:T(8,128)(2,1)}), bf16[1024,512]{1,0:T(8,128)(2,1)}) %all-gather.2.cloned.1.call-update) | async-done | bytes 1048592 | tf_op jit(solution)/shard_map/all_gather | solution.py:36
  53.6 6.2 %while.11 = (s32[]{:T(128)}, f32[512,64]{0,1:T(8,128)S(1)}, f32[512]{0:T(512)S(1)}, bf16[2,512,512]{2,1,0:T(8,128)(2,1)}, bf16[512,512]{1,0:T(8,128)(2,1)S(1)}, ...) while((s32[]{:T(128)}, f32[512,64]{0,1:T(8,128)S(1)}, f32[512]{0:T(512)S(1)}, ...), condition=%wide.region_3.4_spmd.clone, body=%wide.region_1.3_spmd.clone.sunk | while | flops 304152064 | bytes 1973347 | solution.py:50
  53.6 1.2 multiply_reduce_fusion.3
  54.8 1.8 fusion.47
  56.6 1.2 multiply_reduce_fusion.3
  57.9 1.8 fusion.47
  59.7 0.6 copy-done.2
  60.4 18.5 %reduce-scatter.2.cloned.1.call-done = f32[128,64]{0,1:T(8,128)} async-done(((f32[512,64]{0,1:T(8,128)}), f32[128,64]{0,1:T(8,128)}) %reduce-scatter.2.cloned.1.call-update) | async-done | bytes 32784 | tf_op jit(solution)/shard_map/reduce_scatter | solution.py:51
  78.9 0.9 convolution_bitcast_fusion
  79.8 39.4 %psum.14 = f32[64,64]{0,1:T(8,128)S(1)} all-reduce(f32[64,64]{0,1:T(8,128)S(1)} %convolution_bitcast_fusion), channel_id=1, replica_groups=mesh['row'=4,'col'=8] {'row','col'}, use_global_device_ids=true, to_apply=%region_5.6 | all-reduce | flops 4096 | bytes 32768 | tf_op jit(solution)/shard_map/psum | solution.py:52
  119.3 0.1 copy.5
  119.3 5.8 %cholesky.44 = f32[64,64]{1,0:T(8,128)S(1)} custom-call(f32[64,64]{1,0:T(8,128)S(1)} %fusion.30), custom_call_target="Cholesky" | custom-call | tf_op jit(solution)/shard_map/jit(cholesky)/cholesky | solution.py:53
  125.2 0.6 compare_reduce_fusion.1
  125.9 0.7 fusion.23
  126.5 4.9 %custom-call.7 = f32[1,64,64]{1,2,0:T(8,128)S(1)} custom-call(f32[1,64,64]{2,1,0:T(8,128)S(1)} %fusion.23), custom_call_target="InvertDiagBlocksLowerTriangular" | custom-call | tf_op jit(solution)/shard_map/jit(_solve_triangular)/triangular_solve | solution.py:54
  131.5 0.2 fusion.27
  131.7 0.2 fusion.33
  131.9 0.6 multiply_bitcast_fusion
  132.5 41.0 %psum.15 = f32[64,64]{0,1:T(8,128)S(1)} all-reduce(f32[64,64]{0,1:T(8,128)S(1)} %fusion.33), channel_id=1, replica_groups=mesh['row'=4,'col'=8] {'row','col'}, use_global_device_ids=true, to_apply=%region_8.11 | all-reduce | flops 4096 | bytes 32768 | tf_op jit(solution)/shard_map/psum | solution.py:55
  173.5 0.1 copy.7
  173.6 5.8 %cholesky.55 = f32[64,64]{1,0:T(8,128)S(1)} custom-call(f32[64,64]{1,0:T(8,128)S(1)} %fusion.26), custom_call_target="Cholesky" | custom-call | tf_op jit(solution)/shard_map/jit(cholesky)/cholesky | solution.py:56
  179.5 0.6 compare_reduce_fusion
  180.2 0.7 fusion.24
  180.8 4.9 %custom-call.8 = f32[1,64,64]{1,2,0:T(8,128)S(1)} custom-call(f32[1,64,64]{2,1,0:T(8,128)S(1)} %fusion.24), custom_call_target="InvertDiagBlocksLowerTriangular" | custom-call | tf_op jit(solution)/shard_map/jit(_solve_triangular)/triangular_solve | solution.py:57
  185.7 0.9 fusion.22
  (13 shorter events, 0.2 us)
Async XLA Ops:
  7.2 0.8 copy-start.3
  7.2 46.4 %all-gather.2.cloned.1.call-start = ((), (), s32[]{:S(2)}) async-start(), calls=%async_computation.1 | async-start | bytes 1179648 | tf_op jit(solution)/shard_map/all_gather | solution.py:36
  7.9 71.0 %reduce-scatter.2.cloned.1.call-start = ((), (), s32[]{:S(2)}) async-start(), calls=%async_computation.2 | async-start | bytes 163840 | tf_op jit(solution)/shard_map/reduce_scatter | solution.py:51
  36.2 0.9 copy-start
  59.7 0.6 copy-start.2
  125.9 5.6 %copy-start.1 = (f32[128,64]{0,1:T(8,128)S(1)}, f32[128,64]{0,1:T(8,128)}, u32[]{:S(2)}) copy-start(f32[128,64]{0,1:T(8,128)} %reduce-scatter.2.cloned.1.call-done) | copy-start | bytes 98308
Sparse Core Ops, SparseCore 0:
  10.1 43.4 all-gather.1
  60.5 18.3 reduce-scatter.1
where the time goes:
time: 194 us; the launch traced here: 193 us
  blocking collectives  116 us (60%)
  waiting for transfers between devices  28.3 us (15%)
  other arithmetic  27.4 us (14%)
  between operations  14.2 us (7%)
  matrix products  5.88 us (3%)
    psum x1, blocking collectives, per_device(): gram_two = lax.psum(product_of(first, first), ('row', 'col'))  41 us
    psum x1, blocking collectives, per_device(): lax.psum(product_of(sketch.astype(jnp.float32), sketched), ('row', 'col'))  39.4 us
    all_gather x1, blocking collectives, per_device(): tests = lax.all_gather(sketch, 'col', axis=0, tiled=True)  28.2 us
    reduce_scatter x1, waiting for transfers between devices, per_device(): sketched = lax.psum_scatter(total, 'row', scatter_dimension=0, tiled=True)  18.5 us
    all_gather x1, waiting for transfers between devices, per_device(): points = lax.all_gather(embeddings, 'col', axis=0, tiled=True)  9.11 us
    all_gather x1, blocking collectives, per_device(): own_points = lax.all_gather(embeddings, 'row', axis=0, tiled=True)  7.18 us
    another operation x3, other arithmetic, per_device(): lower_two = jnp.linalg.cholesky(gram_two)  6.52 us
    another operation x3, other arithmetic, per_device(): lower = jnp.linalg.cholesky(core)  6.52 us
  transfers between devices with their start and end apart: 2, of which 2 were waited for; matrix products, arithmetic and copies ran while one was open for 0% of the time, Pallas kernels for 0%

commit v1 on v0

--- a/solution.py
+++ b/solution.py
@@ -2,6 +2,10 @@
 import jax.numpy as jnp
 from jax import lax
 from jax.sharding import PartitionSpec as P
+
+
+def load_arrays(in_array):
+    return lax.psum(lax.psum(in_array, "row"), "col")
 
 
 def squares_of(points):
@@ -49,7 +53,7 @@
     )
     total, unused = lax.scan(step, total, stacked)
     sketched = lax.psum_scatter(total, "row", scatter_dimension=0, tiled=True)
-    core = lax.psum(product_of(sketch.astype(jnp.float32), sketched), ("row", "col"))
+    core = load_arrays(product_of(sketch.astype(jnp.float32), sketched))
     lower = jnp.linalg.cholesky(core)
     first = jax.scipy.linalg.solve_triangular(lower, sketched.T, lower=True).T
     gram_two = lax.psum(product_of(first, first), ("row", "col"))

time: 194 us -> 199 us (1.026)
  blocking collectives: 116 us -> 120 us
    psum x1 -> x2, blocking collectives: 39.4 us -> 47.5 us  [load_arrays(): return lax.psum(lax.psum(in_array, 'row'), 'col')]
    psum x1, blocking collectives: 41 us -> 36.9 us  [per_device(): gram_two = lax.psum(product_of(first, first), ('row', 'col'))]
where the time goes in v1:
time: 199 us; the launch traced here: 197 us
  blocking collectives  120 us (60%)
  waiting for transfers between devices  28.3 us (14%)
  other arithmetic  27.4 us (14%)
  between operations  14.2 us (7%)
  matrix products  5.88 us (3%)
    psum x2, blocking collectives, load_arrays(): return lax.psum(lax.psum(in_array, 'row'), 'col')  47.5 us
    psum x1, blocking collectives, per_device(): gram_two = lax.psum(product_of(first, first), ('row', 'col'))  36.9 us
    all_gather x1, blocking collectives, per_device(): tests = lax.all_gather(sketch, 'col', axis=0, tiled=True)  28.2 us
    reduce_scatter x1, waiting for transfers between devices, per_device(): sketched = lax.psum_scatter(total, 'row', scatter_dimension=0, tiled=True)  18.5 us
    all_gather x1, waiting for transfers between devices, per_device(): points = lax.all_gather(embeddings, 'col', axis=0, tiled=True)  9.11 us
    all_gather x1, blocking collectives, per_device(): own_points = lax.all_gather(embeddings, 'row', axis=0, tiled=True)  7.18 us
    another operation x3, other arithmetic, per_device(): lower = jnp.linalg.cholesky(core)  6.52 us
    another operation x3, other arithmetic, per_device(): lower_two = jnp.linalg.cholesky(gram_two)  6.52 us
  transfers between devices with their start and end apart: 2, of which 2 were waited for; matrix products, arithmetic and copies ran while one was open for 0% of the time, Pallas kernels for 0%

profile of v1, /device:TPU:0, one launch (start us, length us, event | category | flops | bytes accessed | tf_op | source)
XLA Modules:
  0.0 197.4 jit_solution(5714222830586120763)
XLA Ops:
  7.2 0.7 all-gather.2.cloned.1.call-update
  8.0 28.2 %all_gather.11 = bf16[1024,64]{0,1:T(8,128)(2,1)S(1)} all-gather(bf16[128,64]{0,1:T(8,128)(2,1)S(1)} %copy-done.3), channel_id=1, replica_groups=mesh['row'=4,'col'=8] {'col'}, dimensions={0}, use_global_device_ids=true | all-gather | bytes 147456 | tf_op jit(solution)/shard_map/all_gather | solution.py:41
  36.2 0.2 copy.4
  36.4 0.7 copy-done
  37.1 7.2 %all_gather.9 = bf16[512,512]{1,0:T(8,128)(2,1)S(1)} all-gather(bf16[128,512]{1,0:T(8,128)(2,1)S(1)} %copy-done), channel_id=1, replica_groups=mesh['row'=4,'col'=8] {'row'}, dimensions={0}, use_global_device_ids=true | all-gather | bytes 655360 | tf_op jit(solution)/shard_map/all_gather | solution.py:36
  44.3 0.2 multiply_reduce_fusion.1
  44.5 9.1 %all-gather.2.cloned.1.call-done = bf16[1024,512]{1,0:T(8,128)(2,1)} async-done(((bf16[128,512]{1,0:T(8,128)(2,1)}), bf16[1024,512]{1,0:T(8,128)(2,1)}) %all-gather.2.cloned.1.call-update) | async-done | bytes 1048592 | tf_op jit(solution)/shard_map/all_gather | solution.py:40
  53.6 6.2 %while.11 = (s32[]{:T(128)}, f32[512,64]{0,1:T(8,128)S(1)}, f32[512]{0:T(512)S(1)}, bf16[2,512,512]{2,1,0:T(8,128)(2,1)}, bf16[512,512]{1,0:T(8,128)(2,1)S(1)}, ...) while((s32[]{:T(128)}, f32[512,64]{0,1:T(8,128)S(1)}, f32[512]{0:T(512)S(1)}, ...), condition=%wide.region_3.4_spmd.clone, body=%wide.region_1.3_spmd.clone.sunk | while | flops 304152064 | bytes 1973347 | solution.py:54
  53.6 1.2 multiply_reduce_fusion.3
  54.8 1.8 fusion.47
  56.6 1.2 multiply_reduce_fusion.3
  57.9 1.8 fusion.47
  59.7 0.6 copy-done.2
  60.4 18.5 %reduce-scatter.2.cloned.1.call-done = f32[128,64]{0,1:T(8,128)} async-done(((f32[512,64]{0,1:T(8,128)}), f32[128,64]{0,1:T(8,128)}) %reduce-scatter.2.cloned.1.call-update) | async-done | bytes 32784 | tf_op jit(solution)/shard_map/reduce_scatter | solution.py:55
  78.9 0.9 convolution_bitcast_fusion
  79.8 10.3 %psum.21 = f32[64,64]{0,1:T(8,128)S(1)} all-reduce(f32[64,64]{0,1:T(8,128)S(1)} %convolution_bitcast_fusion), channel_id=1, replica_groups=mesh['row'=4,'col'=8] {'row'}, use_global_device_ids=true, to_apply=%region_5.6 | all-reduce | flops 4096 | bytes 32768 | tf_op jit(solution)/shard_map/psum | solution.py:8
  90.1 37.2 %psum.22 = f32[64,64]{0,1:T(8,128)S(1)} all-reduce(f32[64,64]{0,1:T(8,128)S(1)} %psum.21), channel_id=1, replica_groups=mesh['row'=4,'col'=8] {'col'}, use_global_device_ids=true, to_apply=%region_6.7 | all-reduce | flops 4096 | bytes 32768 | tf_op jit(solution)/shard_map/psum | solution.py:8
  127.3 0.1 copy.5
  127.4 5.8 %cholesky.44 = f32[64,64]{1,0:T(8,128)S(1)} custom-call(f32[64,64]{1,0:T(8,128)S(1)} %fusion.30), custom_call_target="Cholesky" | custom-call | tf_op jit(solution)/shard_map/jit(cholesky)/cholesky | solution.py:57
  133.3 0.6 compare_reduce_fusion.1
  133.9 0.7 fusion.23
  134.6 4.9 %custom-call.7 = f32[1,64,64]{1,2,0:T(8,128)S(1)} custom-call(f32[1,64,64]{2,1,0:T(8,128)S(1)} %fusion.23), custom_call_target="InvertDiagBlocksLowerTriangular" | custom-call | tf_op jit(solution)/shard_map/jit(_solve_triangular)/triangular_solve | solution.py:58
  139.5 0.2 fusion.27
  139.8 0.2 fusion.33
  140.0 0.6 multiply_bitcast_fusion
  140.6 36.9 %psum.23 = f32[64,64]{0,1:T(8,128)S(1)} all-reduce(f32[64,64]{0,1:T(8,128)S(1)} %fusion.33), channel_id=1, replica_groups=mesh['row'=4,'col'=8] {'row','col'}, use_global_device_ids=true, to_apply=%region_9.12 | all-reduce | flops 4096 | bytes 32768 | tf_op jit(solution)/shard_map/psum | solution.py:59
  177.5 0.1 copy.7
  177.6 5.8 %cholesky.55 = f32[64,64]{1,0:T(8,128)S(1)} custom-call(f32[64,64]{1,0:T(8,128)S(1)} %fusion.26), custom_call_target="Cholesky" | custom-call | tf_op jit(solution)/shard_map/jit(cholesky)/cholesky | solution.py:60
  183.5 0.6 compare_reduce_fusion
  184.1 0.7 fusion.24
  184.8 4.9 %custom-call.8 = f32[1,64,64]{1,2,0:T(8,128)S(1)} custom-call(f32[1,64,64]{2,1,0:T(8,128)S(1)} %fusion.24), custom_call_target="InvertDiagBlocksLowerTriangular" | custom-call | tf_op jit(solution)/shard_map/jit(_solve_triangular)/triangular_solve | solution.py:61
  189.7 0.9 fusion.22
  (14 shorter events, 0.2 us)
Async XLA Ops:
  7.2 0.8 copy-start.3
  7.2 46.4 %all-gather.2.cloned.1.call-start = ((), (), s32[]{:S(2)}) async-start(), calls=%async_computation.1 | async-start | bytes 1179648 | tf_op jit(solution)/shard_map/all_gather | solution.py:40
  7.9 71.0 %reduce-scatter.2.cloned.1.call-start = ((), (), s32[]{:S(2)}) async-start(), calls=%async_computation.2 | async-start | bytes 163840 | tf_op jit(solution)/shard_map/reduce_scatter | solution.py:55
  36.2 0.9 copy-start
  59.7 0.6 copy-start.2
  133.9 5.6 %copy-start.1 = (f32[128,64]{0,1:T(8,128)S(1)}, f32[128,64]{0,1:T(8,128)}, u32[]{:S(2)}) copy-start(f32[128,64]{0,1:T(8,128)} %reduce-scatter.2.cloned.1.call-done) | copy-start | bytes 98308
Sparse Core Ops, SparseCore 0:
  10.1 43.4 all-gather.1
  60.5 18.3 reduce-scatter.1
